TPU v7x, 32 devices: a whole 2x2x4 slice. The times are simulated.
32 devices in a mesh: groups: 2 (over y), seq: 4 (over z), head: 2 (over x), tile: 2 (over core).
Axes of the slice: x: 2, y: 2, z: 4, core: 2. Of those that a mesh axis runs over, the one named last changes fastest.
Arguments:
- query_states: bfloat16 [4608, 3072], P(('groups', 'seq', 'tile'), 'head'), parts along dimension 0, may hold values from -5 to 5
- key_states: bfloat16 [4608, 3072], P(('groups', 'seq', 'tile'), 'head'), parts along dimension 0, may hold values from -5 to 5
- value_states: bfloat16 [4608, 3072], P(('groups', 'seq', 'tile'), 'head'), parts along dimension 0, may hold values from -6 to 6
- residual: bfloat16 [4608, 3072], P(('groups', 'seq', 'tile'), 'head'), parts along dimension 0, may hold values from -6 to 6
- out_weight: bfloat16 [3072, 3072], P(None, 'head'), may hold values from -0.109375 to 0.109375
- gate_scale: float32 [6144], P(('groups', 'head')), parts along dimension 0, may hold values from 2 to 8
Outputs:
- block_out: bfloat16 [4608, 3072], P(('groups', 'seq', 'tile'), 'head'), parts along dimension 0
There are 2 independent parts, one for each index of `groups`. A program takes and returns all parts, laid end to end along the dimension named above; an argument that names none is the same for every part. Nothing has to cross between parts.
All inputs are finite; a program needn't handle non-finite values.
Results may differ from a plain program's by a relative error of at most 0.0065.
Values may be sent and summed in bfloat16 or wider, within the bound.
A program may use at most 128 MiB of HBM per device.

v0:
```python
import math

import jax
import jax.numpy as jnp
from jax import lax
from jax.sharding import PartitionSpec as P

HD = 128


def per_device(query_states, key_states, value_states, residual, out_weight, gate_scale):
    row_count = query_states.shape[0]
    heads_here = query_states.shape[1] // HD
    score_scale = 1.0 / math.sqrt(HD)
    query_heads = query_states.reshape(row_count, heads_here, HD)
    running_max = jnp.full((heads_here, row_count), -jnp.inf, jnp.float32)
    denominator = jnp.zeros((heads_here, row_count), jnp.float32)
    numerator = jnp.zeros((row_count, heads_here, HD), jnp.float32)
    key_heads = lax.all_gather(key_states, ("seq", "tile"), axis=0, tiled=True).reshape(
        -1, heads_here, HD
    )
    value_heads = lax.all_gather(value_states, ("seq", "tile"), axis=0, tiled=True).reshape(
        -1, heads_here, HD
    )
    scores = (
        jnp.einsum("qhd,khd->hqk", query_heads, key_heads, preferred_element_type=jnp.float32)
        * score_scale
    )
    new_max = jnp.max(scores, axis=2)
    shrink = jnp.exp(running_max - new_max)
    weights = jnp.exp(scores - new_max[:, :, None])
    denominator = denominator * shrink + jnp.sum(weights, axis=2)
    probs = weights.astype(jnp.bfloat16)
    numerator = numerator * shrink.T[:, :, None] + jnp.einsum(
        "hqk,khd->qhd", probs, value_heads, preferred_element_type=jnp.float32
    )
    running_max, denominator, numerator = (new_max, denominator, numerator)
    attended = (
        (numerator / denominator.T[:, :, None])
        .astype(jnp.bfloat16)
        .reshape(row_count, heads_here * HD)
    )
    projected = jnp.dot(
        lax.all_gather(attended, "head", axis=1, tiled=True),
        out_weight,
        preferred_element_type=jnp.float32,
    )
    return (residual.astype(jnp.float32) + gate_scale[None, :] * projected).astype(jnp.bfloat16)


def solution(mesh):
    placed = (
        P(("groups", "seq", "tile"), "head"),
        P(("groups", "seq", "tile"), "head"),
        P(("groups", "seq", "tile"), "head"),
        P(("groups", "seq", "tile"), "head"),
        P(None, "head"),
        P(("groups", "head")),
    )
    return jax.shard_map(
        per_device,
        mesh=mesh,
        in_specs=placed,
        out_specs=P(("groups", "seq", "tile"), "head"),
        check_vma=False,
    )
```

profile of v0, /device:TPU:0, one launch (start us, length us, event | category | flops | bytes accessed | tf_op | source)
XLA Modules:
  0.0 223.8 jit_solution(13114338873008730694)
XLA Ops:
  6.5 0.0 copy-start
  6.5 0.0 all-gather.4.cloned.1.call-start
  6.5 0.7 all-gather.4.cloned.1.call-update
  7.3 0.0 all-gather.6.cloned.1.call-start
  7.3 0.7 all-gather.6.cloned.1.call-update
  8.0 0.0 all-gather.8.cloned.1.call-start
  8.1 74.9 %all-gather.4.cloned.1.call-done = bf16[2304,1536]{1,0:T(8,128)(2,1)} async-done(((bf16[288,1536]{1,0:T(8,128)(2,1)}), bf16[2304,1536]{1,0:T(8,128)(2,1)}) %all-gather.4.cloned.1.call-update) | async-done | bytes 7077904 | tf_op jit(solution)/shard_map/all_gather | solution.py:19
  83.0 10.3 %copy.14 = bf16[2304,1536]{0,1:T(8,128)(2,1)} copy(bf16[2304,1536]{1,0:T(8,128)(2,1)} %all-gather.4.cloned.1.call-done) | data formatting | bytes 14155776 | tf_op jit(solution)/shard_map/all_gather | solution.py:19
  93.3 0.0 copy-done
  93.3 14.8 %multiply_reduce_fusion = (f32[12,288]{1,0:T(8,128)S(1)}, f32[12,288,2304]{2,1,0:T(8,128)}) fusion(bf16[2304,12,128]{0,2,1:T(8,128)(2,1)} %bitcast.34, bf16[288,1536]{1,0:T(8,128)(2,1)S(1)} %copy-done), kind=kOutput, calls=%fused_computation.1 | convolution fusion | flops 2054353536 | bytes 39826944 | tf_op jit(solution)/shard_map/qhd,khd->hqk/dot_general | solution.py:26
  108.2 14.0 %fusion = f32[12,288]{1,0:T(8,128)S(1)} fusion(f32[12,288,2304]{2,1,0:T(8,128)} %get-tuple-element.6, f32[12,288]{1,0:T(8,128)S(1)} %get-tuple-element.5), kind=kLoop, calls=%fused_computation.2 | loop fusion | flops 23884416 | bytes 31878144 | tf_op jit(solution)/shard_map/reduce_sum | solution.py:32
  122.2 32.4 %all-gather.6.cloned.1.call-done = bf16[2304,1536]{1,0:T(8,128)(2,1)} async-done(((bf16[288,1536]{1,0:T(8,128)(2,1)}), bf16[2304,1536]{1,0:T(8,128)(2,1)}) %all-gather.6.cloned.1.call-update) | async-done | bytes 7077904 | tf_op jit(solution)/shard_map/all_gather | solution.py:22
  154.5 10.3 %copy.17 = bf16[2304,1536]{0,1:T(8,128)(2,1)} copy(bf16[2304,1536]{1,0:T(8,128)(2,1)} %all-gather.6.cloned.1.call-done) | data formatting | bytes 14155776 | tf_op jit(solution)/shard_map/all_gather | solution.py:22
  164.8 0.0 copy-start.2
  164.8 0.0 copy-start.3
  164.8 15.1 %fusion.12 = bf16[12,36,8,128]{3,2,1,0:T(8,128)(2,1)S(1)} fusion(bf16[2304,12,128]{0,2,1:T(8,128)(2,1)} %bitcast.35, f32[12,288,2304]{2,1,0:T(8,128)} %get-tuple-element.6, f32[12,288]{1,0:T(8,128)S(1)} %get-tuple-element.5, f32[288,12]{0,1:T(8,128)S(1)} %bitcast_add_fusion.1, f32[288,12]{0,1:T(8,128)S(1)} %multiply_bitcast_fusion), kind=kOutput, calls=%fused_computation.13 | convolution fusion | flops 2063646720 | bytes 39854592 | tf_op jit(solution)/shard_map/hqk,khd->qhd/dot_general | solution.py:34
  179.9 1.1 copy.31
  181.0 0.0 all-gather.8.cloned.1.call-update
  181.0 28.2 %all-gather.8.cloned.1.call-done = bf16[288,3072]{1,0:T(8,128)(2,1)} async-done(((bf16[288,1536]{1,0:T(8,128)(2,1)}), bf16[288,3072]{1,0:T(8,128)(2,1)}) %all-gather.8.cloned.1.call-update) | async-done | bytes 1769488 | tf_op jit(solution)/shard_map/all_gather | solution.py:44
  209.2 0.0 copy-done.2
  209.2 0.0 copy-done.3
  209.2 0.0 copy-start.1
  209.2 8.1 %fusion.7 = bf16[288,1536]{1,0:T(8,128)(2,1)} fusion(bf16[288,3072]{1,0:T(8,128)(2,1)} %all-gather.8.cloned.1.call-done, bf16[3072,1536]{1,0:T(8,128)(2,1)} %param.10, bf16[288,1536]{1,0:T(8,128)(2,1)S(1)} %copy-done.2, f32[1536]{0:T(1024)S(1)} %copy-done.3), kind=kOutput, calls=%fused_computation.9 | convolution fusion | flops 2719678464 | bytes 12982272 | tf_op jit(solution)/shard_map/dot_general | solution.py:43
  217.3 0.0 copy-done.1
  (2 shorter events, 0.0 us)
Async XLA Ops:
  6.5 86.8 %copy-start = (bf16[288,1536]{1,0:T(8,128)(2,1)S(1)}, bf16[288,1536]{1,0:T(8,128)(2,1)}, u32[]{:S(2)}) copy-start(bf16[288,1536]{1,0:T(8,128)(2,1)} %param.6) | copy-start | bytes 2654212
  6.5 76.5 %all-gather.4.cloned.1.call-start = ((), (), s32[]{:S(2)}) async-start(), calls=%async_computation | async-start | bytes 7962624 | tf_op jit(solution)/shard_map/all_gather | solution.py:19
  7.3 147.3 %all-gather.6.cloned.1.call-start = ((), (), s32[]{:S(2)}) async-start(), calls=%async_computation.1 | async-start | bytes 7962624 | tf_op jit(solution)/shard_map/all_gather | solution.py:22
  8.0 201.2 %all-gather.8.cloned.1.call-start = ((), (), s32[]{:S(2)}) async-start(), calls=%async_computation.2 | async-start | bytes 2654208 | tf_op jit(solution)/shard_map/all_gather | solution.py:44
  164.8 44.4 %copy-start.2 = (bf16[288,1536]{1,0:T(8,128)(2,1)S(1)}, bf16[288,1536]{1,0:T(8,128)(2,1)}, u32[]{:S(2)}) copy-start(bf16[288,1536]{1,0:T(8,128)(2,1)} %param.9) | copy-start | bytes 2654212
  164.8 44.4 %copy-start.3 = (f32[1536]{0:T(1024)S(1)}, f32[1536]{0:T(1024)}, u32[]{:S(2)}) copy-start(f32[1536]{0:T(1024)} %param.11) | copy-start | bytes 18436
  209.2 8.1 %copy-start.1 = (bf16[288,1536]{1,0:T(8,128)(2,1)S(1)}, bf16[288,1536]{1,0:T(8,128)(2,1)}, u32[]{:S(2)}) copy-start(bf16[288,1536]{1,0:T(8,128)(2,1)} %param.6) | copy-start | bytes 2654212
Sparse Core Ops, SparseCore 0:
  9.0 73.9 all-gather.3
  84.6 69.8 all-gather.5
  181.1 28.0 all-gather.7
where the time goes:
time: 225 us; the launch traced here: 224 us
  waiting for transfers between devices  137 us (61%)
  matrix products  38 us (17%)
  local copies, waits for them, and re-layouts  21.7 us (10%)
  other arithmetic  14 us (6%)
  between operations  13.1 us (6%)
    all_gather x1, waiting for transfers between devices, per_device(): lax.all_gather(key_states, ('seq', 'tile'), axis=0, tiled=True)  74.9 us
    all_gather x1, waiting for transfers between devices, per_device(): lax.all_gather(value_states, ('seq', 'tile'), axis=0, tiled=True)  32.4 us
    all_gather x1, waiting for transfers between devices, per_device(): lax.all_gather(attended, 'head', axis=1, tiled=True)  28.2 us
    dot_general x1, matrix products, per_device(): jnp.einsum('hqk,khd->qhd', probs, value_heads, preferred_element_type=jnp...  15.1 us
    dot_general x1, matrix products, per_device(): jnp.einsum('qhd,khd->hqk', query_heads, key_heads, preferred_element_type...  14.8 us
    reduce_sum x1, other arithmetic, per_device(): denominator = denominator * shrink + jnp.sum(weights, axis=2)  14 us
    all_gather x1, local copies, waits for them, and re-layouts, per_device(): lax.all_gather(key_states, ('seq', 'tile'), axis=0, tiled=True)  10.3 us
    all_gather x1, local copies, waits for them, and re-layouts, per_device(): lax.all_gather(value_states, ('seq', 'tile'), axis=0, tiled=True)  10.3 us
  transfers between devices with their start and end apart: 3, of which 3 were waited for; matrix products, arithmetic and copies ran while one was open for 17% of the time, Pallas kernels for 0%

commit v1 on v0

v1 whole, which is shorter than its diff:
```python
import functools
import math

import jax
import jax.numpy as jnp
from jax import lax
from jax.experimental import pallas as pl
from jax.experimental.pallas import tpu as pltpu
from jax.sharding import PartitionSpec as P

HD = 128
MESH = pl.DeviceIdType.MESH


def gathered(query_states, key_states, value_states, residual, out_weight, gate_scale):
    row_count = query_states.shape[0]
    heads_here = query_states.shape[1] // HD
    score_scale = 1.0 / math.sqrt(HD)
    query_heads = query_states.reshape(row_count, heads_here, HD)
    key_heads = lax.all_gather(key_states, ("seq", "tile"), axis=0, tiled=True).reshape(
        -1, heads_here, HD
    )
    value_heads = lax.all_gather(value_states, ("seq", "tile"), axis=0, tiled=True).reshape(
        -1, heads_here, HD
    )
    scores = (
        jnp.einsum("qhd,khd->hqk", query_heads, key_heads, preferred_element_type=jnp.float32)
        * score_scale
    )
    row_max = jnp.max(scores, axis=2)
    weights = jnp.exp(scores - row_max[:, :, None])
    denominator = jnp.sum(weights, axis=2)
    numerator = jnp.einsum(
        "hqk,khd->qhd",
        weights.astype(jnp.bfloat16),
        value_heads,
        preferred_element_type=jnp.float32,
    )
    attended = (
        (numerator / denominator.T[:, :, None])
        .astype(jnp.bfloat16)
        .reshape(row_count, heads_here * HD)
    )
    projected = jnp.dot(
        lax.all_gather(attended, "head", axis=1, tiled=True),
        out_weight,
        preferred_element_type=jnp.float32,
    )
    return (residual.astype(jnp.float32) + gate_scale[None, :] * projected).astype(jnp.bfloat16)


def kernel(
    n,
    nx,
    per_chip,
    q_hbm,
    k_hbm,
    v_hbm,
    res_hbm,
    w_hbm,
    gate_ref,
    out_ref,
    q_out,
    kv_out,
    q_in,
    kv_in,
    o_out,
    att,
    w_buf,
    res_buf,
    acc,
    load_sem,
    w_sem,
    res_sem,
    q_send,
    q_recv,
    kv_send,
    kv_recv,
    fwd_send,
    fwd_recv,
    o_send,
    o_recv,
    x_send,
    x_recv,
):
    z = lax.axis_index("seq")
    x = lax.axis_index("head")
    c = lax.axis_index("tile")
    rows = q_hbm.shape[0]
    columns = w_hbm.shape[1]
    heads_here = n * per_chip

    def ahead(d):
        return lax.rem(z + d, n)

    def behind(d):
        return lax.rem(z - d + n, n)

    def x_ahead(f):
        return lax.rem(x + f, nx)

    def x_behind(f):
        return lax.rem(x - f + nx, nx)

    def slot(s):
        return pl.ds(s * rows, rows)

    loads = {}
    for j in range(per_chip):
        for d in range(n):
            cols = pl.ds(pl.multiple_of((ahead(d) * per_chip + j) * HD, HD), HD)
            if d == 0:
                dsts = (q_in.at[j, 0], kv_in.at[j, 0, slot(0)], kv_in.at[j, 1, slot(0)])
            else:
                dsts = (q_out.at[j, d], kv_out.at[j, d, 0], kv_out.at[j, d, 1])
            for t, (src, dst) in enumerate(zip((q_hbm, k_hbm, v_hbm), dsts)):
                copy = pltpu.make_async_copy(src.at[:, cols], dst, load_sem.at[t, j, d])
                copy.start()
                loads[t, j, d] = copy

    barrier = pltpu.get_barrier_semaphore()
    for d in range(1, n):
        pl.semaphore_signal(barrier, inc=1, device_id={"seq": ahead(d)}, device_id_type=MESH)
    for f in range(1, nx):
        pl.semaphore_signal(barrier, inc=1, device_id={"head": x_ahead(f)}, device_id_type=MESH)
    pl.semaphore_signal(barrier, inc=1, device_id={"tile": 1 - c}, device_id_type=MESH)
    pl.semaphore_wait(barrier, n + nx - 1)

    def q_copy(j, d):
        return pltpu.make_async_remote_copy(
            src_ref=q_out.at[j, d],
            dst_ref=q_in.at[j, d],
            send_sem=q_send.at[j, d],
            recv_sem=q_recv.at[j, d],
            device_id={"seq": ahead(d)},
            device_id_type=MESH,
        )

    def kv_copy(j, d):
        return pltpu.make_async_remote_copy(
            src_ref=kv_out.at[j, d],
            dst_ref=kv_in.at[j, :, slot(2 * d)],
            send_sem=kv_send.at[j, d],
            recv_sem=kv_recv.at[j, d],
            device_id={"seq": ahead(d)},
            device_id_type=MESH,
        )

    def fwd_copy(j, d):
        return pltpu.make_async_remote_copy(
            src_ref=kv_in.at[j, :, slot(2 * d)],
            dst_ref=kv_in.at[j, :, slot(2 * d + 1)],
            send_sem=fwd_send.at[j, d],
            recv_sem=fwd_recv.at[j, d],
            device_id={"tile": 1 - c},
            device_id_type=MESH,
        )

    def o_copy(j, d):
        return pltpu.make_async_remote_copy(
            src_ref=o_out.at[j, d],
            dst_ref=att.at[j, d],
            send_sem=o_send.at[j, d],
            recv_sem=o_recv.at[j, d],
            device_id={"seq": behind(d)},
            device_id_type=MESH,
        )

    def x_copy(j, f, d):
        return pltpu.make_async_remote_copy(
            src_ref=att.at[j, d],
            dst_ref=att.at[j, f * n + d],
            send_sem=x_send.at[j, f, d],
            recv_sem=x_recv.at[j, f, d],
            device_id={"head": x_ahead(f)},
            device_id_type=MESH,
        )

    for j in range(per_chip):
        for d in range(n - 1, 0, -1):
            loads[1, j, d].wait()
            loads[2, j, d].wait()
            kv_copy(j, d).start()
            loads[0, j, d].wait()
            q_copy(j, d).start()
        for t in range(3):
            loads[t, j, 0].wait()
        fwd_copy(j, 0).start()

    w_loads = {}
    for j in range(per_chip):
        for f in range(nx):
            for d in range(n):
                head = x_behind(f) * heads_here + ahead(d) * per_chip + j
                copy = pltpu.make_async_copy(
                    w_hbm.at[pl.ds(pl.multiple_of(head * HD, HD), HD)],
                    w_buf.at[j, pl.ds((f * n + d) * HD, HD)],
                    w_sem.at[j, f * n + d],
                )
                copy.start()
                w_loads[j, f, d] = copy
    res_load = pltpu.make_async_copy(res_hbm, res_buf, res_sem)
    res_load.start()

    factor = math.log2(math.e) / math.sqrt(HD)

    def attend(j, d):
        scores = lax.dot_general(
            q_in[j, d],
            kv_in[j, 0],
            (((1,), (1,)), ((), ())),
            preferred_element_type=jnp.float32,
        )
        row_max = jnp.max(scores, axis=1, keepdims=True)
        weights = jnp.exp2((scores - row_max) * factor)
        denominator = jnp.sum(weights, axis=1, keepdims=True)
        numerator = jnp.dot(
            weights.astype(jnp.bfloat16), kv_in[j, 1], preferred_element_type=jnp.float32
        )
        return (numerator / denominator).astype(jnp.bfloat16)

    def relay(j):
        for d in range(n):
            if d:
                o_copy(j, d).wait_recv()
            for f in range(1, nx):
                x_copy(j, f, d).start()

    width = math.gcd(columns, 512)

    def project(j):
        for f in range(nx):
            for d in range(n):
                w_loads[j, f, d].wait()
                if f:
                    x_copy(j, f, d).wait_recv()
        if j == per_chip - 1:
            res_load.wait()
        rows_in = jnp.concatenate([att[j, s] for s in range(nx * n)], axis=1)
        for start in range(0, columns, width):
            cols = slice(start, start + width)
            part = jnp.dot(rows_in, w_buf[j, :, cols], preferred_element_type=jnp.float32)
            if j:
                part += acc[:, cols]
            if j < per_chip - 1:
                acc[:, cols] = part
            else:
                out_ref[:, cols] = (
                    res_buf[:, cols].astype(jnp.float32) + gate_ref[:, cols] * part
                ).astype(jnp.bfloat16)

    for j in range(per_chip):
        for d in range(1, n):
            kv_copy(j, d).wait_recv()
            fwd_copy(j, d).start()
        for d in range(n):
            fwd_copy(j, d).wait_recv()
        for d in range(1, n):
            q_copy(j, d).wait_recv()
        if j:
            relay(j - 1)

        def step(i, carry):
            d = n - 1 - i
            o_out[j, d] = attend(j, d)

            @pl.when(d > 0)
            def _():
                o_copy(j, d).start()

            return carry

        lax.fori_loop(0, n, step, 0)
        att[j, 0] = o_out[j, 0]
        if j:
            project(j - 1)
    relay(per_chip - 1)
    project(per_chip - 1)

    for j in range(per_chip):
        for d in range(n):
            fwd_copy(j, d).wait_send()
            if d:
                q_copy(j, d).wait_send()
                kv_copy(j, d).wait_send()
                o_copy(j, d).wait_send()
            for f in range(1, nx):
                x_copy(j, f, d).wait_send()


def exchanged(n, nx, query_states, key_states, value_states, residual, out_weight, gate_scale):
    rows, width = query_states.shape
    columns = out_weight.shape[1]
    per_chip = width // HD // n
    bf16 = jnp.bfloat16
    dma = pltpu.SemaphoreType.DMA
    anywhere = pl.BlockSpec(memory_space=pl.ANY)
    in_vmem = pl.BlockSpec(memory_space=pltpu.VMEM)
    return pl.pallas_call(
        functools.partial(kernel, n, nx, per_chip),
        out_shape=jax.ShapeDtypeStruct((rows, columns), bf16),
        in_specs=[anywhere] * 5 + [in_vmem],
        out_specs=in_vmem,
        scratch_shapes=[
            pltpu.VMEM((per_chip, n, rows, HD), bf16),
            pltpu.VMEM((per_chip, n, 2, rows, HD), bf16),
            pltpu.VMEM((per_chip, n, rows, HD), bf16),
            pltpu.VMEM((per_chip, 2, 2 * n * rows, HD), bf16),
            pltpu.VMEM((per_chip, n, rows, HD), bf16),
            pltpu.VMEM((per_chip, nx * n, rows, HD), bf16),
            pltpu.VMEM((per_chip, nx * n * HD, columns), bf16),
            pltpu.VMEM((rows, columns), bf16),
            pltpu.VMEM((rows, columns), jnp.float32),
            dma((3, per_chip, n)),
            dma((per_chip, nx * n)),
            dma,
            dma((per_chip, n)),
            dma((per_chip, n)),
            dma((per_chip, n)),
            dma((per_chip, n)),
            dma((per_chip, n)),
            dma((per_chip, n)),
            dma((per_chip, n)),
            dma((per_chip, n)),
            dma((per_chip, nx, n)),
            dma((per_chip, nx, n)),
        ],
        compiler_params=pltpu.CompilerParams(
            collective_id=0, has_side_effects=True, vmem_limit_bytes=56 << 20
        ),
    )(query_states, key_states, value_states, residual, out_weight, gate_scale[None, :])


def solution(mesh):
    n, nx = mesh.shape["seq"], mesh.shape["head"]

    def per_device(query_states, *rest):
        heads_here = query_states.shape[1] // HD
        if heads_here % n or mesh.shape["tile"] != 2:
            return gathered(query_states, *rest)
        return exchanged(n, nx, query_states, *rest)

    placed = (
        P(("groups", "seq", "tile"), "head"),
        P(("groups", "seq", "tile"), "head"),
        P(("groups", "seq", "tile"), "head"),
        P(("groups", "seq", "tile"), "head"),
        P(None, "head"),
        P(("groups", "head")),
    )
    return jax.shard_map(
        per_device,
        mesh=mesh,
        in_specs=placed,
        out_specs=P(("groups", "seq", "tile"), "head"),
        check_vma=False,
    )
```

time: 225 us -> 105 us (0.47)
  waiting for transfers between devices: 137 us -> 0 us
  Pallas kernels: 0 us -> 101 us
  matrix products: 38 us -> 0 us
  local copies, waits for them, and re-layouts: 21.7 us -> 3.43 us
  other arithmetic: 14 us -> 0 us
  between operations: 13.1 us -> 0.01 us
    all_gather x3 -> x0, waiting for transfers between devices: 135 us -> none  [the longest x1 74.9 us: per_device(): lax.all_gather(key_states, ('seq', 'tile'), axis=0, tiled=True)]
    pallas_call x0 -> x1, Pallas kernels: none -> 101 us  [exchanged(): pl.pallas_call(functools.partial(kernel, n, nx, per_chip), out_shape=jax....]
    dot_general x3 -> x0, matrix products: 38 us -> none  [the longest x1 15.1 us: per_device(): jnp.einsum('hqk,khd->qhd', probs, value_heads, preferred_element_type=jnp...]
    all_gather x2 -> x0, local copies, waits for them, and re-layouts: 20.6 us -> none  [the longest x1 10.3 us: per_device(): lax.all_gather(key_states, ('seq', 'tile'), axis=0, tiled=True)]
    reduce_sum x1 -> x0, other arithmetic: 14 us -> none  [per_device(): denominator = denominator * shrink + jnp.sum(weights, axis=2)]
  transfers between devices with their start and end apart: 3 -> 0, of which waited for: 3 -> 0; matrix products, arithmetic and copies ran while one was open for 17% -> 0% of each run, Pallas kernels for 0% -> 0%
where the time goes in v1:
time: 105 us
  Pallas kernels  101 us (96%)
  local copies, waits for them, and re-layouts  3.43 us (3%)
    pallas_call x1, Pallas kernels, exchanged(): pl.pallas_call(functools.partial(kernel, n, nx, per_chip), out_shape=jax....  101 us
    unnamed x1, local copies, waits for them, and re-layouts  2.14 us

profile of v1, /device:TPU:0, one launch (start us, length us, event | category | flops | bytes accessed | tf_op | source)
XLA Modules:
  0.0 104.6 jit_solution(2060037116454238361)
XLA Ops:
  0.0 1.3 %broadcast_in_dim.3.gate_ref = f32[1,1536]{1,0:T(1,128)} reshape(f32[1536]{0:T(1024)} %param.11) | data formatting | bytes 12288 | tf_op jit(solution)/shard_map/broadcast_in_dim | solution.py:331
  1.3 101.2 %shard_map.64 = bf16[288,1536]{1,0:T(8,128)(2,1)} custom-call(bf16[288,1536]{1,0:T(8,128)(2,1)} %q_hbm.1, bf16[288,1536]{1,0:T(8,128)(2,1)} %k_hbm.1, bf16[288,1536]{1,0:T(8,128)(2,1)} %v_hbm.1, bf16[288,1536]{1,0:T(8,128)(2,1)} %res_hbm.1, bf16[3072,1536]{1,0:T(8,128)(2,1)} %w_hbm.1, f32[1,1536]{1,0:T(1,128)} %broadcast_in_dim.3.gate_ref), custom_call_target="tpu_custom_call" | custom-call | tf_op jit(solution)/shard_map/pallas_call | solution.py:299
  102.5 2.1 %copy.8 = bf16[288,1536]{1,0:T(8,128)(2,1)} copy(bf16[288,1536]{1,0:T(8,128)(2,1)} %shard_map.64) | data formatting | bytes 1769472

commit v2 on v1

--- a/solution.py
+++ b/solution.py
@@ -56,9 +56,7 @@
     q_hbm,
     k_hbm,
     v_hbm,
-    res_hbm,
     w_hbm,
-    gate_ref,
     out_ref,
     q_out,
     kv_out,
@@ -67,11 +65,8 @@
     o_out,
     att,
     w_buf,
-    res_buf,
-    acc,
     load_sem,
     w_sem,
-    res_sem,
     q_send,
     q_recv,
     kv_send,
@@ -89,12 +84,11 @@
     rows = q_hbm.shape[0]
     columns = w_hbm.shape[1]
     heads_here = n * per_chip
-
-    def ahead(d):
-        return lax.rem(z + d, n)
-
-    def behind(d):
-        return lax.rem(z - d + n, n)
+    bits = [1 << b for b in range(n.bit_length() - 1)]
+    order = list(range(n - 1, 0, -1))
+
+    def partner(d):
+        return sum(b * (((z // b) + (d // b)) % 2) for b in bits)
 
     def x_ahead(f):
         return lax.rem(x + f, nx)
@@ -108,7 +102,7 @@
     loads = {}
     for j in range(per_chip):
         for d in range(n):
-            cols = pl.ds(pl.multiple_of((ahead(d) * per_chip + j) * HD, HD), HD)
+            cols = pl.ds(pl.multiple_of((partner(d) * per_chip + j) * HD, HD), HD)
             if d == 0:
                 dsts = (q_in.at[j, 0], kv_in.at[j, 0, slot(0)], kv_in.at[j, 1, slot(0)])
             else:
@@ -120,7 +114,7 @@
 
     barrier = pltpu.get_barrier_semaphore()
     for d in range(1, n):
-        pl.semaphore_signal(barrier, inc=1, device_id={"seq": ahead(d)}, device_id_type=MESH)
+        pl.semaphore_signal(barrier, inc=1, device_id={"seq": partner(d)}, device_id_type=MESH)
     for f in range(1, nx):
         pl.semaphore_signal(barrier, inc=1, device_id={"head": x_ahead(f)}, device_id_type=MESH)
     pl.semaphore_signal(barrier, inc=1, device_id={"tile": 1 - c}, device_id_type=MESH)
@@ -132,7 +126,7 @@
             dst_ref=q_in.at[j, d],
             send_sem=q_send.at[j, d],
             recv_sem=q_recv.at[j, d],
-            device_id={"seq": ahead(d)},
+            device_id={"seq": partner(d)},
             device_id_type=MESH,
         )
 
@@ -142,7 +136,7 @@
             dst_ref=kv_in.at[j, :, slot(2 * d)],
             send_sem=kv_send.at[j, d],
             recv_sem=kv_recv.at[j, d],
-            device_id={"seq": ahead(d)},
+            device_id={"seq": partner(d)},
             device_id_type=MESH,
         )
 
@@ -162,7 +156,7 @@
             dst_ref=att.at[j, d],
             send_sem=o_send.at[j, d],
             recv_sem=o_recv.at[j, d],
-            device_id={"seq": behind(d)},
+            device_id={"seq": partner(d)},
             device_id_type=MESH,
         )
 
@@ -176,22 +170,29 @@
             device_id_type=MESH,
         )
 
-    for j in range(per_chip):
-        for d in range(n - 1, 0, -1):
+    def send_kv(j):
+        for d in order:
             loads[1, j, d].wait()
             loads[2, j, d].wait()
             kv_copy(j, d).start()
-            loads[0, j, d].wait()
-            q_copy(j, d).start()
         for t in range(3):
             loads[t, j, 0].wait()
         fwd_copy(j, 0).start()
+
+    def send_q(j):
+        for d in order:
+            loads[0, j, d].wait()
+            q_copy(j, d).start()
+
+    for j in range(min(2, per_chip)):
+        send_kv(j)
+        send_q(j)
 
     w_loads = {}
     for j in range(per_chip):
         for f in range(nx):
             for d in range(n):
-                head = x_behind(f) * heads_here + ahead(d) * per_chip + j
+                head = x_behind(f) * heads_here + partner(d) * per_chip + j
                 copy = pltpu.make_async_copy(
                     w_hbm.at[pl.ds(pl.multiple_of(head * HD, HD), HD)],
                     w_buf.at[j, pl.ds((f * n + d) * HD, HD)],
@@ -199,8 +200,6 @@
                 )
                 copy.start()
                 w_loads[j, f, d] = copy
-    res_load = pltpu.make_async_copy(res_hbm, res_buf, res_sem)
-    res_load.start()
 
     factor = math.log2(math.e) / math.sqrt(HD)
 
@@ -220,9 +219,8 @@
         return (numerator / denominator).astype(jnp.bfloat16)
 
     def relay(j):
-        for d in range(n):
-            if d:
-                o_copy(j, d).wait_recv()
+        for d in order:
+            o_copy(j, d).wait_recv()
             for f in range(1, nx):
                 x_copy(j, f, d).start()
 
@@ -234,44 +232,37 @@
                 w_loads[j, f, d].wait()
                 if f:
                     x_copy(j, f, d).wait_recv()
-        if j == per_chip - 1:
-            res_load.wait()
         rows_in = jnp.concatenate([att[j, s] for s in range(nx * n)], axis=1)
         for start in range(0, columns, width):
             cols = slice(start, start + width)
             part = jnp.dot(rows_in, w_buf[j, :, cols], preferred_element_type=jnp.float32)
-            if j:
-                part += acc[:, cols]
-            if j < per_chip - 1:
-                acc[:, cols] = part
-            else:
-                out_ref[:, cols] = (
-                    res_buf[:, cols].astype(jnp.float32) + gate_ref[:, cols] * part
-                ).astype(jnp.bfloat16)
+            out_ref[:, cols] = out_ref[:, cols] + part if j else part
 
     for j in range(per_chip):
-        for d in range(1, n):
+        for d in order:
             kv_copy(j, d).wait_recv()
             fwd_copy(j, d).start()
+        if j and j + 1 < per_chip:
+            send_kv(j + 1)
         for d in range(n):
             fwd_copy(j, d).wait_recv()
-        for d in range(1, n):
-            q_copy(j, d).wait_recv()
-        if j:
+        att[j, 0] = attend(j, 0)
+        for f in range(1, nx):
+            x_copy(j, f, 0).start()
+        if j and j + 1 == per_chip:
             relay(j - 1)
 
         def step(i, carry):
             d = n - 1 - i
+            q_copy(j, d).wait_recv()
             o_out[j, d] = attend(j, d)
-
-            @pl.when(d > 0)
-            def _():
-                o_copy(j, d).start()
-
+            o_copy(j, d).start()
             return carry
 
-        lax.fori_loop(0, n, step, 0)
-        att[j, 0] = o_out[j, 0]
+        lax.fori_loop(0, n - 1, step, 0)
+        if j and j + 1 < per_chip:
+            send_q(j + 1)
+            relay(j - 1)
         if j:
             project(j - 1)
     relay(per_chip - 1)
@@ -288,7 +279,7 @@
                 x_copy(j, f, d).wait_send()
 
 
-def exchanged(n, nx, query_states, key_states, value_states, residual, out_weight, gate_scale):
+def exchanged(n, nx, query_states, key_states, value_states, out_weight):
     rows, width = query_states.shape
     columns = out_weight.shape[1]
     per_chip = width // HD // n
@@ -298,8 +289,8 @@
     in_vmem = pl.BlockSpec(memory_space=pltpu.VMEM)
     return pl.pallas_call(
         functools.partial(kernel, n, nx, per_chip),
-        out_shape=jax.ShapeDtypeStruct((rows, columns), bf16),
-        in_specs=[anywhere] * 5 + [in_vmem],
+        out_shape=jax.ShapeDtypeStruct((rows, columns), jnp.float32),
+        in_specs=[anywhere] * 4,
         out_specs=in_vmem,
         scratch_shapes=[
             pltpu.VMEM((per_chip, n, rows, HD), bf16),
@@ -309,11 +300,8 @@
             pltpu.VMEM((per_chip, n, rows, HD), bf16),
             pltpu.VMEM((per_chip, nx * n, rows, HD), bf16),
             pltpu.VMEM((per_chip, nx * n * HD, columns), bf16),
-            pltpu.VMEM((rows, columns), bf16),
-            pltpu.VMEM((rows, columns), jnp.float32),
             dma((3, per_chip, n)),
             dma((per_chip, nx * n)),
-            dma,
             dma((per_chip, n)),
             dma((per_chip, n)),
             dma((per_chip, n)),
@@ -328,17 +316,22 @@
         compiler_params=pltpu.CompilerParams(
             collective_id=0, has_side_effects=True, vmem_limit_bytes=56 << 20
         ),
-    )(query_states, key_states, value_states, residual, out_weight, gate_scale[None, :])
+    )(query_states, key_states, value_states, out_weight)
 
 
 def solution(mesh):
     n, nx = mesh.shape["seq"], mesh.shape["head"]
 
-    def per_device(query_states, *rest):
+    def per_device(query_states, key_states, value_states, residual, out_weight, gate_scale):
         heads_here = query_states.shape[1] // HD
-        if heads_here % n or mesh.shape["tile"] != 2:
-            return gathered(query_states, *rest)
-        return exchanged(n, nx, query_states, *rest)
+        if heads_here % n or n & (n - 1) or mesh.shape["tile"] != 2:
+            return gathered(
+                query_states, key_states, value_states, residual, out_weight, gate_scale
+            )
+        projected = exchanged(n, nx, query_states, key_states, value_states, out_weight)
+        return (residual.astype(jnp.float32) + gate_scale[None, :] * projected).astype(
+            jnp.bfloat16
+        )
 
     placed = (
         P(("groups", "seq", "tile"), "head"),

time: 105 us -> 95.9 us (0.913)
  Pallas kernels: 101 us -> 93.1 us
  local copies, waits for them, and re-layouts: 3.43 us -> 0.01 us
  other arithmetic: 0 us -> 2.63 us
    pallas_call x1, Pallas kernels: 101 us -> 93.1 us  [exchanged(): pl.pallas_call(functools.partial(kernel, n, nx, per_chip), out_shape=jax....]
    convert_element_type x0 -> x1, other arithmetic: none -> 2.63 us  [per_device(): (residual.astype(jnp.float32) + gate_scale[None, :] * projected).astype(j...]
    unnamed x1 -> x4, local copies, waits for them, and re-layouts: 2.14 us -> 0.01 us
    broadcast_in_dim x1 -> x0, local copies, waits for them, and re-layouts: 1.29 us -> none  [exchanged(): gate_scale[None, :]]
where the time goes in v2:
time: 95.9 us; the launch traced here: 95.8 us
  Pallas kernels  93.1 us (97%)
  other arithmetic  2.63 us (3%)
    pallas_call x1, Pallas kernels, exchanged(): pl.pallas_call(functools.partial(kernel, n, nx, per_chip), out_shape=jax....  93.1 us
    convert_element_type x1, other arithmetic, per_device(): (residual.astype(jnp.float32) + gate_scale[None, :] * projected).astype(j...  2.63 us

profile of v2, /device:TPU:0, one launch (start us, length us, event | category | flops | bytes accessed | tf_op | source)
XLA Modules:
  0.0 95.8 jit_solution(5777572488999578682)
XLA Ops:
  0.0 0.0 copy-start.1
  0.0 0.0 copy-start
  0.0 93.1 %shard_map.64 = f32[288,1536]{1,0:T(8,128)} custom-call(bf16[288,1536]{1,0:T(8,128)(2,1)} %q_hbm.1, bf16[288,1536]{1,0:T(8,128)(2,1)} %k_hbm.1, bf16[288,1536]{1,0:T(8,128)(2,1)} %v_hbm.1, bf16[3072,1536]{1,0:T(8,128)(2,1)} %w_hbm.1), custom_call_target="tpu_custom_call" | custom-call | tf_op jit(solution)/shard_map/pallas_call | solution.py:290
  93.1 0.0 copy-done.1
  93.2 0.0 copy-done
  93.2 2.6 %add_convert_fusion = bf16[288,1536]{1,0:T(8,128)(2,1)} fusion(f32[288,1536]{1,0:T(8,128)} %shard_map.64, bf16[288,1536]{1,0:T(8,128)(2,1)S(1)} %copy-done, f32[1536]{0:T(1024)S(1)} %copy-done.1), kind=kLoop, calls=%fused_computation | loop fusion | flops 1769472 | bytes 3545088 | tf_op jit(solution)/shard_map/convert_element_type | solution.py:332
Async XLA Ops:
  0.0 93.1 %copy-start.1 = (f32[1536]{0:T(1024)S(1)}, f32[1536]{0:T(1024)}, u32[]{:S(2)}) copy-start(f32[1536]{0:T(1024)} %param.11) | copy-start | bytes 18436
  0.0 93.2 %copy-start = (bf16[288,1536]{1,0:T(8,128)(2,1)S(1)}, bf16[288,1536]{1,0:T(8,128)(2,1)}, u32[]{:S(2)}) copy-start(bf16[288,1536]{1,0:T(8,128)(2,1)} %param.9) | copy-start | bytes 2654212

commit v3 on v2

--- a/solution.py
+++ b/solution.py
@@ -85,7 +85,8 @@
     columns = w_hbm.shape[1]
     heads_here = n * per_chip
     bits = [1 << b for b in range(n.bit_length() - 1)]
-    order = list(range(n - 1, 0, -1))
+    order = [0] + [n - 2, n - 1] * (n > 2) + list(range(1, n - 2 * (n > 2)))
+    last = per_chip - 1
 
     def partner(d):
         return sum(b * (((z // b) + (d // b)) % 2) for b in bits)
@@ -101,7 +102,7 @@
 
     loads = {}
     for j in range(per_chip):
-        for d in range(n):
+        for d in order[1:] + [0]:
             cols = pl.ds(pl.multiple_of((partner(d) * per_chip + j) * HD, HD), HD)
             if d == 0:
                 dsts = (q_in.at[j, 0], kv_in.at[j, 0, slot(0)], kv_in.at[j, 1, slot(0)])
@@ -150,28 +151,28 @@
             device_id_type=MESH,
         )
 
-    def o_copy(j, d):
+    def o_copy(j, p, d):
         return pltpu.make_async_remote_copy(
             src_ref=o_out.at[j, d],
-            dst_ref=att.at[j, d],
+            dst_ref=att.at[j, p * nx],
             send_sem=o_send.at[j, d],
             recv_sem=o_recv.at[j, d],
             device_id={"seq": partner(d)},
             device_id_type=MESH,
         )
 
-    def x_copy(j, f, d):
-        return pltpu.make_async_remote_copy(
-            src_ref=att.at[j, d],
-            dst_ref=att.at[j, f * n + d],
-            send_sem=x_send.at[j, f, d],
-            recv_sem=x_recv.at[j, f, d],
+    def x_copy(j, f, p):
+        return pltpu.make_async_remote_copy(
+            src_ref=att.at[j, p * nx],
+            dst_ref=att.at[j, p * nx + f],
+            send_sem=x_send.at[j, f, p],
+            recv_sem=x_recv.at[j, f, p],
             device_id={"head": x_ahead(f)},
             device_id_type=MESH,
         )
 
     def send_kv(j):
-        for d in order:
+        for d in order[1:]:
             loads[1, j, d].wait()
             loads[2, j, d].wait()
             kv_copy(j, d).start()
@@ -180,7 +181,7 @@
         fwd_copy(j, 0).start()
 
     def send_q(j):
-        for d in order:
+        for d in order[1:]:
             loads[0, j, d].wait()
             q_copy(j, d).start()
 
@@ -190,16 +191,16 @@
 
     w_loads = {}
     for j in range(per_chip):
-        for f in range(nx):
-            for d in range(n):
+        for p, d in enumerate(order):
+            for f in range(nx):
                 head = x_behind(f) * heads_here + partner(d) * per_chip + j
                 copy = pltpu.make_async_copy(
                     w_hbm.at[pl.ds(pl.multiple_of(head * HD, HD), HD)],
-                    w_buf.at[j, pl.ds((f * n + d) * HD, HD)],
-                    w_sem.at[j, f * n + d],
+                    w_buf.at[j, pl.ds((p * nx + f) * HD, HD)],
+                    w_sem.at[j, p * nx + f],
                 )
                 copy.start()
-                w_loads[j, f, d] = copy
+                w_loads[j, p, f] = copy
 
     factor = math.log2(math.e) / math.sqrt(HD)
 
@@ -218,55 +219,65 @@
         )
         return (numerator / denominator).astype(jnp.bfloat16)
 
-    def relay(j):
-        for d in order:
-            o_copy(j, d).wait_recv()
+    def relay(j, places=range(1, n)):
+        for p in places:
+            o_copy(j, p, order[p]).wait_recv()
             for f in range(1, nx):
-                x_copy(j, f, d).start()
+                x_copy(j, f, p).start()
 
     width = math.gcd(columns, 512)
 
-    def project(j):
-        for f in range(nx):
-            for d in range(n):
-                w_loads[j, f, d].wait()
+    def project(j, low=0, high=n):
+        for p in range(low, high):
+            for f in range(nx):
+                w_loads[j, p, f].wait()
                 if f:
-                    x_copy(j, f, d).wait_recv()
-        rows_in = jnp.concatenate([att[j, s] for s in range(nx * n)], axis=1)
+                    x_copy(j, f, p).wait_recv()
+        rows_in = jnp.concatenate([att[j, s] for s in range(low * nx, high * nx)], axis=1)
         for start in range(0, columns, width):
             cols = slice(start, start + width)
-            part = jnp.dot(rows_in, w_buf[j, :, cols], preferred_element_type=jnp.float32)
-            out_ref[:, cols] = out_ref[:, cols] + part if j else part
+            part = jnp.dot(
+                rows_in,
+                w_buf[j, low * nx * HD : high * nx * HD, cols],
+                preferred_element_type=jnp.float32,
+            )
+            out_ref[:, cols] = out_ref[:, cols] + part if j or low else part
 
     for j in range(per_chip):
-        for d in order:
+        for d in order[1:]:
             kv_copy(j, d).wait_recv()
             fwd_copy(j, d).start()
-        if j and j + 1 < per_chip:
+        if j and j < last:
             send_kv(j + 1)
         for d in range(n):
             fwd_copy(j, d).wait_recv()
         att[j, 0] = attend(j, 0)
         for f in range(1, nx):
             x_copy(j, f, 0).start()
-        if j and j + 1 == per_chip:
+        if j and j == last:
             relay(j - 1)
 
         def step(i, carry):
-            d = n - 1 - i
+            d = 1 + (n - 3 + i) % (n - 1) if n > 2 else 1
             q_copy(j, d).wait_recv()
             o_out[j, d] = attend(j, d)
-            o_copy(j, d).start()
+            o_copy(j, i + 1, d).start()
             return carry
 
         lax.fori_loop(0, n - 1, step, 0)
-        if j and j + 1 < per_chip:
+        if j and j < last:
             send_q(j + 1)
             relay(j - 1)
-        if j:
+        if j and j < last:
             project(j - 1)
-    relay(per_chip - 1)
-    project(per_chip - 1)
+    if last:
+        relay(last, range(1, 2))
+        project(last - 1)
+        relay(last, range(2, n))
+    else:
+        relay(last)
+    project(last, 0, n - 1)
+    project(last, n - 1, n)
 
     for j in range(per_chip):
         for d in range(n):
@@ -274,7 +285,7 @@
             if d:
                 q_copy(j, d).wait_send()
                 kv_copy(j, d).wait_send()
-                o_copy(j, d).wait_send()
+                o_copy(j, order.index(d), d).wait_send()
             for f in range(1, nx):
                 x_copy(j, f, d).wait_send()
 

time: 95.9 us -> 94.4 us (0.984)
  Pallas kernels: 93.1 us -> 91.6 us
    pallas_call x1, Pallas kernels: 93.1 us -> 91.6 us  [exchanged(): pl.pallas_call(functools.partial(kernel, n, nx, per_chip), out_shape=jax....]
where the time goes in v3:
time: 94.4 us; the launch traced here: 94.3 us
  Pallas kernels  91.6 us (97%)
  other arithmetic  2.63 us (3%)
    pallas_call x1, Pallas kernels, exchanged(): pl.pallas_call(functools.partial(kernel, n, nx, per_chip), out_shape=jax....  91.6 us
    convert_element_type x1, other arithmetic, per_device(): (residual.astype(jnp.float32) + gate_scale[None, :] * projected).astype(j...  2.63 us

profile of v3, /device:TPU:0, one launch (start us, length us, event | category | flops | bytes accessed | tf_op | source)
XLA Modules:
  0.0 94.3 jit_solution(3561225231603240906)
XLA Ops:
  0.0 0.0 copy-start.1
  0.0 0.0 copy-start
  0.0 91.6 %shard_map.64 = f32[288,1536]{1,0:T(8,128)} custom-call(bf16[288,1536]{1,0:T(8,128)(2,1)} %q_hbm.1, bf16[288,1536]{1,0:T(8,128)(2,1)} %k_hbm.1, bf16[288,1536]{1,0:T(8,128)(2,1)} %v_hbm.1, bf16[3072,1536]{1,0:T(8,128)(2,1)} %w_hbm.1), custom_call_target="tpu_custom_call" | custom-call | tf_op jit(solution)/shard_map/pallas_call | solution.py:301
  91.6 0.0 copy-done.1
  91.6 0.0 copy-done
  91.7 2.6 %add_convert_fusion = bf16[288,1536]{1,0:T(8,128)(2,1)} fusion(f32[288,1536]{1,0:T(8,128)} %shard_map.64, bf16[288,1536]{1,0:T(8,128)(2,1)S(1)} %copy-done, f32[1536]{0:T(1024)S(1)} %copy-done.1), kind=kLoop, calls=%fused_computation | loop fusion | flops 1769472 | bytes 3545088 | tf_op jit(solution)/shard_map/convert_element_type | solution.py:343
Async XLA Ops:
  0.0 91.6 %copy-start.1 = (f32[1536]{0:T(1024)S(1)}, f32[1536]{0:T(1024)}, u32[]{:S(2)}) copy-start(f32[1536]{0:T(1024)} %param.11) | copy-start | bytes 18436
  0.0 91.6 %copy-start = (bf16[288,1536]{1,0:T(8,128)(2,1)S(1)}, bf16[288,1536]{1,0:T(8,128)(2,1)}, u32[]{:S(2)}) copy-start(bf16[288,1536]{1,0:T(8,128)(2,1)} %param.9) | copy-start | bytes 2654212

commit v4 on v3

--- a/solution.py
+++ b/solution.py
@@ -57,6 +57,8 @@
     k_hbm,
     v_hbm,
     w_hbm,
+    res_hbm,
+    gate_hbm,
     out_ref,
     q_out,
     kv_out,
@@ -65,8 +67,12 @@
     o_out,
     att,
     w_buf,
+    res_buf,
+    gate_buf,
+    acc,
     load_sem,
     w_sem,
+    end_sem,
     q_send,
     q_recv,
     kv_send,
@@ -202,6 +208,13 @@
                 copy.start()
                 w_loads[j, p, f] = copy
 
+    ends = [
+        pltpu.make_async_copy(res_hbm, res_buf, end_sem.at[0]),
+        pltpu.make_async_copy(gate_hbm, gate_buf, end_sem.at[1]),
+    ]
+    for copy in ends:
+        copy.start()
+
     factor = math.log2(math.e) / math.sqrt(HD)
 
     def attend(j, d):
@@ -241,7 +254,14 @@
                 w_buf[j, low * nx * HD : high * nx * HD, cols],
                 preferred_element_type=jnp.float32,
             )
-            out_ref[:, cols] = out_ref[:, cols] + part if j or low else part
+            total = acc[:, cols] + part if j or low else part
+            if j == last and high == n:
+                gate = gate_buf[cols].reshape(1, width)
+                out_ref[:, cols] = (
+                    res_buf[:, cols].astype(jnp.float32) + gate * total
+                ).astype(jnp.bfloat16)
+            else:
+                acc[:, cols] = total
 
     for j in range(per_chip):
         for d in order[1:]:
@@ -254,19 +274,27 @@
         att[j, 0] = attend(j, 0)
         for f in range(1, nx):
             x_copy(j, f, 0).start()
-        if j and j == last:
-            relay(j - 1)
+
+        follow = j and j < last
+        if follow:
+            for d in order[1:]:
+                loads[0, j + 1, d].wait()
 
         def step(i, carry):
             d = 1 + (n - 3 + i) % (n - 1) if n > 2 else 1
+            if j and j == last:
+                o_copy(j - 1, i + 1, d).wait_recv()
+                for f in range(1, nx):
+                    x_copy(j - 1, f, i + 1).start()
             q_copy(j, d).wait_recv()
             o_out[j, d] = attend(j, d)
             o_copy(j, i + 1, d).start()
+            if follow:
+                q_copy(j + 1, d).start()
             return carry
 
         lax.fori_loop(0, n - 1, step, 0)
         if j and j < last:
-            send_q(j + 1)
             relay(j - 1)
         if j and j < last:
             project(j - 1)
@@ -277,6 +305,8 @@
     else:
         relay(last)
     project(last, 0, n - 1)
+    for copy in ends:
+        copy.wait()
     project(last, n - 1, n)
 
     for j in range(per_chip):
@@ -290,7 +320,7 @@
                 x_copy(j, f, d).wait_send()
 
 
-def exchanged(n, nx, query_states, key_states, value_states, out_weight):
+def exchanged(n, nx, query_states, key_states, value_states, out_weight, residual, gate_scale):
     rows, width = query_states.shape
     columns = out_weight.shape[1]
     per_chip = width // HD // n
@@ -300,8 +330,8 @@
     in_vmem = pl.BlockSpec(memory_space=pltpu.VMEM)
     return pl.pallas_call(
         functools.partial(kernel, n, nx, per_chip),
-        out_shape=jax.ShapeDtypeStruct((rows, columns), jnp.float32),
-        in_specs=[anywhere] * 4,
+        out_shape=jax.ShapeDtypeStruct((rows, columns), bf16),
+        in_specs=[anywhere] * 6,
         out_specs=in_vmem,
         scratch_shapes=[
             pltpu.VMEM((per_chip, n, rows, HD), bf16),
@@ -311,8 +341,12 @@
             pltpu.VMEM((per_chip, n, rows, HD), bf16),
             pltpu.VMEM((per_chip, nx * n, rows, HD), bf16),
             pltpu.VMEM((per_chip, nx * n * HD, columns), bf16),
+            pltpu.VMEM((rows, columns), bf16),
+            pltpu.VMEM((columns,), jnp.float32),
+            pltpu.VMEM((rows, columns), jnp.float32),
             dma((3, per_chip, n)),
             dma((per_chip, nx * n)),
+            dma((2,)),
             dma((per_chip, n)),
             dma((per_chip, n)),
             dma((per_chip, n)),
@@ -327,7 +361,7 @@
         compiler_params=pltpu.CompilerParams(
             collective_id=0, has_side_effects=True, vmem_limit_bytes=56 << 20
         ),
-    )(query_states, key_states, value_states, out_weight)
+    )(query_states, key_states, value_states, out_weight, residual, gate_scale)
 
 
 def solution(mesh):
@@ -339,9 +373,8 @@
             return gathered(
                 query_states, key_states, value_states, residual, out_weight, gate_scale
             )
-        projected = exchanged(n, nx, query_states, key_states, value_states, out_weight)
-        return (residual.astype(jnp.float32) + gate_scale[None, :] * projected).astype(
-            jnp.bfloat16
+        return exchanged(
+            n, nx, query_states, key_states, value_states, out_weight, residual, gate_scale
         )
 
     placed = (

time: 94.4 us -> 93.5 us (level)
  other arithmetic: 2.63 us -> 0 us
  local copies, waits for them, and re-layouts: 0.01 us -> 2.14 us
    convert_element_type x1 -> x0, other arithmetic: 2.63 us -> none  [per_device(): (residual.astype(jnp.float32) + gate_scale[None, :] * projected).astype(j...]
    unnamed x4 -> x1, local copies, waits for them, and re-layouts: 0.01 us -> 2.14 us
where the time goes in v4:
time: 93.5 us; the launch traced here: 93.3 us
  Pallas kernels  91.2 us (98%)
  local copies, waits for them, and re-layouts  2.14 us (2%)
    pallas_call x1, Pallas kernels, exchanged(): pl.pallas_call(functools.partial(kernel, n, nx, per_chip), out_shape=jax....  91.2 us
    unnamed x1, local copies, waits for them, and re-layouts  2.14 us

profile of v4, /device:TPU:0, one launch (start us, length us, event | category | flops | bytes accessed | tf_op | source)
XLA Modules:
  0.0 93.3 jit_solution(7402394473003857620)
XLA Ops:
  0.0 91.2 %shard_map.64 = bf16[288,1536]{1,0:T(8,128)(2,1)} custom-call(bf16[288,1536]{1,0:T(8,128)(2,1)} %q_hbm.1, bf16[288,1536]{1,0:T(8,128)(2,1)} %k_hbm.1, bf16[288,1536]{1,0:T(8,128)(2,1)} %v_hbm.1, bf16[3072,1536]{1,0:T(8,128)(2,1)} %w_hbm.1, bf16[288,1536]{1,0:T(8,128)(2,1)} %res_hbm.1, f32[1536]{0:T(1024)} %gate_hbm.1), custom_call_target="tpu_custom_call" | custom-call | tf_op jit(solution)/shard_map/pallas_call | solution.py:331
  91.2 2.1 %copy.8 = bf16[288,1536]{1,0:T(8,128)(2,1)} copy(bf16[288,1536]{1,0:T(8,128)(2,1)} %shard_map.64) | data formatting | bytes 1769472
